TPU v7x, 32 devices: a whole 2x2x4 slice. The times are simulated.
32 devices in a mesh: layer: 2 (over y), latent: 8 (over z, x), tok: 2 (over core).
Axes of the slice: x: 2, y: 2, z: 4, core: 2. Of those that a mesh axis runs over, the one named last changes fastest.
Arguments:
- resid: bfloat16 [2, 384, 2304], P('layer', 'tok', 'latent'), may hold values from -6 to 6
- w_enc: bfloat16 [2, 2304, 2048], P('layer', None, 'latent'), may hold values from -0.09375 to 0.09375
- b_enc: float32 [2048], P('latent'), may hold values from -3 to 3
- w_dec: bfloat16 [2, 2048, 2304], P('layer', 'latent'), may hold values from -0.125 to 0.125
- b_dec: bfloat16 [2, 2304], P('layer', 'latent'), may hold values from -3 to 3
Outputs:
- grad_w_enc: bfloat16 [2, 2304, 2048], P('layer', 'tok', 'latent')
- grad_w_dec: bfloat16 [2, 2048, 2304], P('layer', 'latent')
All inputs are finite; a program needn't handle non-finite values.
Results may differ from a plain program's by a relative error of at most 0.023.
Values may be sent and summed in bfloat16 or wider, within the bound.
A program may use at most 64 MiB of HBM per device.

v0:
```python
import jax
import jax.numpy as jnp
from jax import lax
from jax.sharding import PartitionSpec as P

BETA = 4.0


def shards(resid, w_enc, b_enc, w_dec, b_dec):
    decoder = w_dec[0]
    x_full, bias_full = (
        lax.all_gather(resid, "latent", axis=2, tiled=True),
        lax.all_gather(b_dec.reshape(1, 1, -1), "latent", axis=2, tiled=True),
    )
    x_full = x_full[0]
    bias_full = bias_full.reshape(-1).astype(jnp.float32)
    tok_rows = x_full.shape[0]
    tokens = tok_rows * lax.axis_size("tok")
    partial_value = jnp.dot(x_full, w_enc[0], preferred_element_type=jnp.float32)
    pre = lax.psum(partial_value.astype(jnp.bfloat16), "layer").astype(jnp.float32) + b_enc
    act = (jax.nn.softplus(BETA * pre) / BETA).astype(jnp.bfloat16)
    slope = jax.nn.sigmoid(BETA * pre)
    recon = lax.psum(
        jnp.dot(act, decoder, preferred_element_type=jnp.float32).astype(jnp.bfloat16), "latent"
    ).astype(jnp.float32)
    grad_all = (2.0 / tokens * (recon + bias_full - x_full.astype(jnp.float32))).astype(
        jnp.bfloat16
    )
    dec_sum = lax.dot_general(
        act, grad_all, (((0,), (0,)), ((), ())), preferred_element_type=jnp.float32
    )
    rows_grad = lax.dot_general(
        grad_all, decoder, (((1,), (1,)), ((), ())), preferred_element_type=jnp.float32
    )
    act_grad = rows_grad
    dec_sum, act_grad = (dec_sum, act_grad)
    grad_act = lax.psum(act_grad.astype(jnp.bfloat16), "layer").astype(jnp.float32)
    grad_pre = (grad_act * slope).astype(jnp.bfloat16)
    grad_w_dec = lax.psum(dec_sum.astype(jnp.bfloat16), "tok")
    grad_w_enc = lax.psum_scatter(
        lax.dot_general(
            x_full, grad_pre, (((0,), (0,)), ((), ())), preferred_element_type=jnp.float32
        ).astype(jnp.bfloat16),
        "tok",
        scatter_dimension=0,
        tiled=True,
    )
    return (grad_w_enc[None], grad_w_dec[None])


def solution(mesh):
    placed = (
        P("layer", "tok", "latent"),
        P("layer", None, "latent"),
        P("latent"),
        P("layer", "latent", None),
        P("layer", "latent"),
    )
    return jax.shard_map(
        shards,
        mesh=mesh,
        in_specs=placed,
        out_specs=(P("layer", "tok", "latent"), P("layer", "latent", None)),
        check_vma=False,
    )
```

profile of v0, /device:TPU:0, one launch (start us, length us, event | category | flops | bytes accessed | tf_op | source)
XLA Modules:
  0.0 235.1 jit_solution(12181217095717214668)
XLA Ops:
  7.2 0.0 copy-start
  7.2 0.0 all-reduce.6.cloned.1.call-start
  7.2 1.9 copy.8
  9.1 51.7 %all_gather.6 = bf16[1,192,2304]{1,0,2:T(2,128)(2,1)S(1)} all-gather(bf16[1,192,288]{1,0,2:T(2,128)(2,1)} %copy.8), channel_id=1, replica_groups=mesh['layer'=2,'latent'=8,'tok'=2] {'latent'}, dimensions={2}, use_global_device_ids=true | all-gather | bytes 995328 | tf_op jit(solution)/shard_map/all_gather | solution.py:12
  60.8 4.9 %copy.9 = bf16[1,192,2304]{2,1,0:T(8,128)(2,1)} copy(bf16[1,192,2304]{1,0,2:T(2,128)(2,1)S(1)} %all_gather.6) | data formatting | bytes 1769472 | tf_op jit(solution)/shard_map/all_gather | solution.py:12
  65.7 2.6 %fusion.7 = bf16[192,256]{1,0:T(8,128)(2,1)} fusion(bf16[1,2304,256]{2,1,0:T(8,128)(2,1)} %param.6, bf16[1,192,2304]{2,1,0:T(8,128)(2,1)} %copy.9), kind=kOutput, calls=%fused_computation.11 | convolution fusion | flops 226541568 | bytes 2162688 | tf_op jit(solution)/shard_map/dot_general | solution.py:19
  68.3 0.0 all-reduce.6.cloned.1.call-update
  68.3 0.0 all-reduce.8.cloned.1.call-start
  68.4 20.0 %all-reduce.6.cloned.1.call-done = bf16[192,256]{1,0:T(8,128)(2,1)} async-done(((bf16[192,256]{1,0:T(8,128)(2,1)}), bf16[192,256]{1,0:T(8,128)(2,1)}) %all-reduce.6.cloned.1.call-update) | async-done | bytes 98320 | tf_op jit(solution)/shard_map/psum | solution.py:20
  88.3 0.0 copy-done
  88.3 2.3 convolution_convert_fusion.2
  90.7 0.0 all-reduce.8.cloned.1.call-update
  90.7 0.0 all-reduce.10.cloned.1.call-start
  90.7 0.6 dynamic-slice
  92.0 0.3 dynamic-update-slice
  92.3 22.1 %all-reduce = bf16[2304]{0:T(1024)(128)(2,1)S(1)} all-reduce(bf16[2304]{0:T(1024)(128)(2,1)S(1)} %dynamic-update-slice), channel_id=2, replica_groups=mesh['layer'=2,'latent'=8,'tok'=2] {'latent'}, use_global_device_ids=true, to_apply=%add | all-reduce | flops 2304 | bytes 9216
  114.4 53.9 %all-reduce.8.cloned.1.call-done = bf16[192,2304]{1,0:T(8,128)(2,1)} async-done(((bf16[192,2304]{1,0:T(8,128)(2,1)}), bf16[192,2304]{1,0:T(8,128)(2,1)}) %all-reduce.8.cloned.1.call-update) | async-done | bytes 884752 | tf_op jit(solution)/shard_map/psum | solution.py:23
  168.3 2.4 %fusion.10 = bf16[192,256]{1,0:T(8,128)(2,1)} fusion(bf16[1,256,2304]{2,1,0:T(8,128)(2,1)S(1)} %copy-done, bf16[192,2304]{1,0:T(8,128)(2,1)} %all-reduce.8.cloned.1.call-done, bf16[1,192,2304]{2,1,0:T(8,128)(2,1)S(1)} %copy-done.1, f32[2304]{0:T(1024)S(1)} %convert_element_type.66), kind=kOutput, calls=%fused_computation.12 | convolution fusion | flops 229195776 | bytes 3056640 | tf_op jit(solution)/shard_map/dot_general | solution.py:32
  170.7 0.0 all-reduce.10.cloned.1.call-update
  170.7 0.0 reduce-scatter.4.cloned.1.call-start
  170.8 20.7 %all-reduce.10.cloned.1.call-done = bf16[192,256]{1,0:T(8,128)(2,1)} async-done(((bf16[192,256]{1,0:T(8,128)(2,1)}), bf16[192,256]{1,0:T(8,128)(2,1)}) %all-reduce.10.cloned.1.call-update) | async-done | bytes 98320 | tf_op jit(solution)/shard_map/psum | solution.py:37
  191.4 1.4 fusion
  192.9 1.4 copy.11
  194.3 0.0 reduce-scatter.4.cloned.1.call-update
  194.3 0.0 all-reduce.12.cloned.1.call-start
  194.4 2.9 %fusion.1 = bf16[1,256,2304]{2,1,0:T(8,128)(2,1)} fusion(bf16[192,2304]{1,0:T(8,128)(2,1)} %all-reduce.8.cloned.1.call-done, bf16[1,192,2304]{2,1,0:T(8,128)(2,1)S(1)} %copy-done.1, f32[2304]{0:T(1024)S(1)} %convert_element_type.66, bf16[192,256]{1,0:T(8,128)(2,1)S(1)} %copy-done.2, f32[256]{0:T(256)S(1)} %copy-done.4), kind=kOutput, calls=%fused_computation.4 | convolution fusion | flops 230277120 | bytes 3057664 | tf_op jit(solution)/shard_map/dot_general | solution.py:29
  197.3 0.0 all-reduce.12.cloned.1.call-update
  197.3 5.7 %reduce-scatter.4.cloned.1.call-done = bf16[1152,256]{1,0:T(8,128)(2,1)} async-done(((bf16[2304,256]{1,0:T(8,128)(2,1)}), bf16[1152,256]{1,0:T(8,128)(2,1)}) %reduce-scatter.4.cloned.1.call-update) | async-done | bytes 589840
  203.0 1.4 copy.12
  204.4 1.1 copy.10
  205.4 20.7 %all-reduce.12.cloned.1.call-done = bf16[1,256,2304]{2,1,0:T(8,128)(2,1)} async-done(((bf16[1,256,2304]{2,1,0:T(8,128)(2,1)}), bf16[1,256,2304]{2,1,0:T(8,128)(2,1)}) %all-reduce.12.cloned.1.call-update) | async-done | bytes 1179664 | tf_op jit(solution)/shard_map/psum | solution.py:39
  226.2 2.4 %copy.18 = bf16[1,256,2304]{2,1,0:T(8,128)(2,1)} copy(bf16[1,256,2304]{2,1,0:T(8,128)(2,1)} %all-reduce.12.cloned.1.call-done) | data formatting | bytes 2359296
  (13 shorter events, 0.0 us)
Async XLA Ops:
  7.2 81.2 %copy-start = (bf16[1,256,2304]{2,1,0:T(8,128)(2,1)S(1)}, bf16[1,256,2304]{2,1,0:T(8,128)(2,1)}, u32[]{:S(2)}) copy-start(bf16[1,256,2304]{2,1,0:T(8,128)(2,1)} %param.8) | copy-start | bytes 3538948
  7.2 81.2 %all-reduce.6.cloned.1.call-start = ((), (), s32[]{:S(2)}) async-start(), calls=%async_computation.1 | async-start | bytes 196608 | tf_op jit(solution)/shard_map/psum | solution.py:20
  65.7 22.7 %copy-start.4 = (f32[256]{0:T(256)S(1)}, f32[256]{0:T(256)}, u32[]{:S(2)}) copy-start(f32[256]{0:T(256)} %param.7) | copy-start | bytes 3076
  68.3 22.5 %copy-start.5 = (u32[32]{0:T(128)S(1)}, u32[32]{0:T(128)}, u32[]{:S(2)}) copy-start(u32[32]{0:T(128)} %constant.17) | copy-start | bytes 388
  68.3 23.7 %copy-start.3 = (bf16[1,288]{1,0:T(2,128)(2,1)S(1)}, bf16[1,288]{1,0:T(2,128)(2,1)}, u32[]{:S(2)}) copy-start(bf16[1,288]{1,0:T(2,128)(2,1)} %param.9) | copy-start | bytes 1732
  68.3 100.0 %copy-start.1 = (bf16[1,192,2304]{2,1,0:T(8,128)(2,1)S(1)}, bf16[1,192,2304]{2,1,0:T(8,128)(2,1)}, u32[]{:S(2)}) copy-start(bf16[1,192,2304]{2,1,0:T(8,128)(2,1)} %copy.9) | copy-start | bytes 2654212
  68.3 100.0 %all-reduce.8.cloned.1.call-start = ((), (), s32[]{:S(2)}) async-start(), calls=%async_computation.2 | async-start | bytes 1769472 | tf_op jit(solution)/shard_map/psum | solution.py:23
  90.7 100.7 %all-reduce.10.cloned.1.call-start = ((), (), s32[]{:S(2)}) async-start(), calls=%async_computation.3 | async-start | bytes 196608 | tf_op jit(solution)/shard_map/psum | solution.py:37
  114.4 77.0 %copy-start.2 = (bf16[192,256]{1,0:T(8,128)(2,1)S(1)}, bf16[192,256]{1,0:T(8,128)(2,1)}, u32[]{:S(2)}) copy-start(bf16[192,256]{1,0:T(8,128)(2,1)} %all-reduce.6.cloned.1.call-done) | copy-start | bytes 294916
  170.7 32.3 %reduce-scatter.4.cloned.1.call-start = ((), (), s32[]{:S(2)}) async-start(), calls=%async_computation.5 | async-start | bytes 1769472
  194.3 31.8 %all-reduce.12.cloned.1.call-start = ((), (), s32[]{:S(2)}) async-start(), calls=%async_computation.4 | async-start | bytes 2359296 | tf_op jit(solution)/shard_map/psum | solution.py:39
Sparse Core Ops, SparseCore 0:
  68.4 19.8 all-reduce.5
  91.8 76.4 all-reduce.7
  171.1 20.2 all-reduce.9
  194.4 8.5 reduce-scatter.3
  205.2 20.9 all-reduce.11
where the time goes:
time: 235 us
  waiting for transfers between devices  121 us (51%)
  blocking collectives  73.7 us (31%)
  between operations  14.5 us (6%)
  local copies, waits for them, and re-layouts  13.9 us (6%)
  matrix products  11.6 us (5%)
    psum x1, waiting for transfers between devices, shards(): lax.psum(jnp.dot(act, decoder, preferred_element_type=jnp.float32).astype...  53.9 us
    all_gather x1, blocking collectives, shards(): lax.all_gather(resid, 'latent', axis=2, tiled=True)  51.7 us
    unnamed x1, blocking collectives  22.1 us
    psum x1, waiting for transfers between devices, shards(): grad_w_dec = lax.psum(dec_sum.astype(jnp.bfloat16), 'tok')  20.7 us
    psum x1, waiting for transfers between devices, shards(): lax.psum(act_grad.astype(jnp.bfloat16), 'layer').astype(jnp.float32)  20.7 us
    psum x1, waiting for transfers between devices, shards(): lax.psum(partial_value.astype(jnp.bfloat16), 'layer').astype(jnp.float32)  20 us
    unnamed x20, local copies, waits for them, and re-layouts  8.98 us
    unnamed x6, waiting for transfers between devices  5.8 us
  transfers between devices with their start and end apart: 5, of which 5 were waited for; matrix products, arithmetic and copies ran while one was open for 3% of the time, Pallas kernels for 0%

commit v1 on v0

--- a/solution.py
+++ b/solution.py
@@ -9,7 +9,7 @@
 def shards(resid, w_enc, b_enc, w_dec, b_dec):
     decoder = w_dec[0]
     x_full, bias_full = (
-        lax.all_gather(resid, "latent", axis=2, tiled=True),
+        jnp.concatenate(lax.all_gather(resid, "latent"), axis=2),
         lax.all_gather(b_dec.reshape(1, 1, -1), "latent", axis=2, tiled=True),
     )
     x_full = x_full[0]

time: 235 us -> 216 us (0.919)
  blocking collectives: 73.7 us -> 57.8 us
  local copies, waits for them, and re-layouts: 13.9 us -> 9.75 us
    all_gather x1, blocking collectives: 51.7 us -> 35.7 us  [shards(): lax.all_gather(resid, 'latent')]
    all_gather x1 -> x0, local copies, waits for them, and re-layouts: 4.88 us -> none  [shards(): lax.all_gather(resid, 'latent', axis=2, tiled=True)]
    unnamed x20 -> x19, local copies, waits for them, and re-layouts: 8.98 us -> 8.17 us
  transfers between devices with their start and end apart: 5 -> 5, of which waited for: 5 -> 5; matrix products, arithmetic and copies ran while one was open for 3% -> 2% of each run, Pallas kernels for 0% -> 0%
where the time goes in v1:
time: 216 us
  waiting for transfers between devices  123 us (57%)
  blocking collectives  57.8 us (27%)
  between operations  14.5 us (7%)
  matrix products  10.2 us (5%)
  local copies, waits for them, and re-layouts  9.75 us (5%)
    psum x1, waiting for transfers between devices, shards(): lax.psum(jnp.dot(act, decoder, preferred_element_type=jnp.float32).astype...  54.2 us
    all_gather x1, blocking collectives, shards(): lax.all_gather(resid, 'latent')  35.7 us
    unnamed x1, blocking collectives  22.1 us
    psum x1, waiting for transfers between devices, shards(): lax.psum(partial_value.astype(jnp.bfloat16), 'layer').astype(jnp.float32)  21.7 us
    psum x1, waiting for transfers between devices, shards(): grad_w_dec = lax.psum(dec_sum.astype(jnp.bfloat16), 'tok')  20.7 us
    psum x1, waiting for transfers between devices, shards(): lax.psum(act_grad.astype(jnp.bfloat16), 'layer').astype(jnp.float32)  20.7 us
    unnamed x19, local copies, waits for them, and re-layouts  8.17 us
    unnamed x6, waiting for transfers between devices  5.83 us
  transfers between devices with their start and end apart: 5, of which 5 were waited for; matrix products, arithmetic and copies ran while one was open for 2% of the time, Pallas kernels for 0%

profile of v1, /device:TPU:0, one launch (start us, length us, event | category | flops | bytes accessed | tf_op | source)
XLA Modules:
  0.0 215.6 jit_solution(6829175169416253188)
XLA Ops:
  7.2 0.0 copy-start
  7.2 0.0 all-reduce.6.cloned.1.call-start
  7.2 35.7 %all-gather = bf16[8,192,288]{2,1,0:T(8,128)(2,1)S(1)} all-gather(bf16[1,192,288]{2,1,0:T(8,128)(2,1)} %param.5), channel_id=2, replica_groups=mesh['layer'=2,'latent'=8,'tok'=2] {'latent'}, dimensions={0}, use_global_device_ids=true | all-gather | bytes 995328 | tf_op jit(solution)/shard_map/all_gather | solution.py:12
  42.9 0.7 copy.9
  43.6 0.9 squeeze_reshape.3
  44.5 2.3 %fusion.7 = bf16[192,256]{1,0:T(8,128)(2,1)} fusion(bf16[192,2304]{1,0:T(8,128)(2,1)S(1)} %squeeze_reshape.3, bf16[1,2304,256]{2,1,0:T(8,128)(2,1)} %param.6), kind=kOutput, calls=%fused_computation.11 | convolution fusion | flops 226541568 | bytes 2162688 | tf_op jit(solution)/shard_map/dot_general | solution.py:19
  46.9 0.0 all-reduce.6.cloned.1.call-update
  46.9 0.0 all-reduce.8.cloned.1.call-start
  47.0 21.7 %all-reduce.6.cloned.1.call-done = bf16[192,256]{1,0:T(8,128)(2,1)} async-done(((bf16[192,256]{1,0:T(8,128)(2,1)}), bf16[192,256]{1,0:T(8,128)(2,1)}) %all-reduce.6.cloned.1.call-update) | async-done | bytes 98320 | tf_op jit(solution)/shard_map/psum | solution.py:20
  68.6 2.3 %convolution_convert_fusion.2 = bf16[192,2304]{1,0:T(8,128)(2,1)} fusion(bf16[1,256,2304]{2,1,0:T(8,128)(2,1)S(1)} %copy-done, bf16[192,256]{1,0:T(8,128)(2,1)} %all-reduce.6.cloned.1.call-done, f32[256]{0:T(256)S(1)} %copy-done.3), kind=kOutput, calls=%fused_computation.2 | convolution fusion | flops 227475456 | bytes 2163712 | tf_op jit(solution)/shard_map/dot_general | solution.py:24
  70.9 0.0 all-reduce.8.cloned.1.call-update
  71.0 0.0 all-reduce.10.cloned.1.call-start
  71.0 0.6 dynamic-slice
  72.3 0.3 dynamic-update-slice
  72.6 22.1 %all-reduce = bf16[2304]{0:T(1024)(128)(2,1)S(1)} all-reduce(bf16[2304]{0:T(1024)(128)(2,1)S(1)} %dynamic-update-slice), channel_id=3, replica_groups=mesh['layer'=2,'latent'=8,'tok'=2] {'latent'}, use_global_device_ids=true, to_apply=%add | all-reduce | flops 2304 | bytes 9216
  94.7 54.2 %all-reduce.8.cloned.1.call-done = bf16[192,2304]{1,0:T(8,128)(2,1)} async-done(((bf16[192,2304]{1,0:T(8,128)(2,1)}), bf16[192,2304]{1,0:T(8,128)(2,1)}) %all-reduce.8.cloned.1.call-update) | async-done | bytes 884752 | tf_op jit(solution)/shard_map/psum | solution.py:23
  148.9 2.4 %fusion.10 = bf16[192,256]{1,0:T(8,128)(2,1)} fusion(bf16[1,256,2304]{2,1,0:T(8,128)(2,1)S(1)} %copy-done, bf16[192,2304]{1,0:T(8,128)(2,1)S(1)} %squeeze_reshape.3, bf16[192,2304]{1,0:T(8,128)(2,1)} %all-reduce.8.cloned.1.call-done, f32[2304]{0:T(1024)S(1)} %convert_element_type.66), kind=kOutput, calls=%fused_computation.12 | convolution fusion | flops 229195776 | bytes 3056640 | tf_op jit(solution)/shard_map/dot_general | solution.py:32
  151.3 0.0 all-reduce.10.cloned.1.call-update
  151.3 0.0 reduce-scatter.4.cloned.1.call-start
  151.4 20.7 %all-reduce.10.cloned.1.call-done = bf16[192,256]{1,0:T(8,128)(2,1)} async-done(((bf16[192,256]{1,0:T(8,128)(2,1)}), bf16[192,256]{1,0:T(8,128)(2,1)}) %all-reduce.10.cloned.1.call-update) | async-done | bytes 98320 | tf_op jit(solution)/shard_map/psum | solution.py:37
  172.0 1.4 fusion
  173.5 1.4 copy.11
  174.9 0.0 reduce-scatter.4.cloned.1.call-update
  174.9 0.0 all-reduce.12.cloned.1.call-start
  175.0 1.1 copy-done.4
  176.1 1.8 fusion.1
  177.8 0.0 all-reduce.12.cloned.1.call-update
  177.8 5.7 %reduce-scatter.4.cloned.1.call-done = bf16[1152,256]{1,0:T(8,128)(2,1)} async-done(((bf16[2304,256]{1,0:T(8,128)(2,1)}), bf16[1152,256]{1,0:T(8,128)(2,1)}) %reduce-scatter.4.cloned.1.call-update) | async-done | bytes 589840
  183.6 1.4 copy.12
  184.9 1.1 copy.10
  186.0 20.7 %all-reduce.12.cloned.1.call-done = bf16[1,256,2304]{2,1,0:T(8,128)(2,1)} async-done(((bf16[1,256,2304]{2,1,0:T(8,128)(2,1)}), bf16[1,256,2304]{2,1,0:T(8,128)(2,1)}) %all-reduce.12.cloned.1.call-update) | async-done | bytes 1179664 | tf_op jit(solution)/shard_map/psum | solution.py:39
  206.8 2.4 %copy.18 = bf16[1,256,2304]{2,1,0:T(8,128)(2,1)} copy(bf16[1,256,2304]{2,1,0:T(8,128)(2,1)} %all-reduce.12.cloned.1.call-done) | data formatting | bytes 2359296
  (13 shorter events, 0.1 us)
Async XLA Ops:
  7.2 61.5 %copy-start = (bf16[1,256,2304]{2,1,0:T(8,128)(2,1)S(1)}, bf16[1,256,2304]{2,1,0:T(8,128)(2,1)}, u32[]{:S(2)}) copy-start(bf16[1,256,2304]{2,1,0:T(8,128)(2,1)} %param.8) | copy-start | bytes 3538948
  7.2 61.5 %all-reduce.6.cloned.1.call-start = ((), (), s32[]{:S(2)}) async-start(), calls=%async_computation.1 | async-start | bytes 196608 | tf_op jit(solution)/shard_map/psum | solution.py:20
  44.5 24.1 %copy-start.3 = (f32[256]{0:T(256)S(1)}, f32[256]{0:T(256)}, u32[]{:S(2)}) copy-start(f32[256]{0:T(256)} %param.7) | copy-start | bytes 3076
  46.9 24.1 %copy-start.5 = (u32[32]{0:T(128)S(1)}, u32[32]{0:T(128)}, u32[]{:S(2)}) copy-start(u32[32]{0:T(128)} %constant.17) | copy-start | bytes 388
  46.9 25.4 %copy-start.2 = (bf16[1,288]{1,0:T(2,128)(2,1)S(1)}, bf16[1,288]{1,0:T(2,128)(2,1)}, u32[]{:S(2)}) copy-start(bf16[1,288]{1,0:T(2,128)(2,1)} %param.9) | copy-start | bytes 1732
  46.9 102.0 %all-reduce.8.cloned.1.call-start = ((), (), s32[]{:S(2)}) async-start(), calls=%async_computation.2 | async-start | bytes 1769472 | tf_op jit(solution)/shard_map/psum | solution.py:23
  71.0 101.1 %all-reduce.10.cloned.1.call-start = ((), (), s32[]{:S(2)}) async-start(), calls=%async_computation.3 | async-start | bytes 196608 | tf_op jit(solution)/shard_map/psum | solution.py:37
  94.7 77.3 %copy-start.1 = (bf16[192,256]{1,0:T(8,128)(2,1)S(1)}, bf16[192,256]{1,0:T(8,128)(2,1)}, u32[]{:S(2)}) copy-start(bf16[192,256]{1,0:T(8,128)(2,1)} %all-reduce.6.cloned.1.call-done) | copy-start | bytes 294916
  151.3 32.3 %reduce-scatter.4.cloned.1.call-start = ((), (), s32[]{:S(2)}) async-start(), calls=%async_computation.5 | async-start | bytes 1769472
  174.9 1.2 copy-start.4
  174.9 31.8 %all-reduce.12.cloned.1.call-start = ((), (), s32[]{:S(2)}) async-start(), calls=%async_computation.4 | async-start | bytes 2359296 | tf_op jit(solution)/shard_map/psum | solution.py:39
Sparse Core Ops, SparseCore 0:
  47.0 21.5 all-reduce.5
  72.7 76.2 all-reduce.7
  151.7 20.2 all-reduce.9
  175.0 8.5 reduce-scatter.3
  185.8 20.9 all-reduce.11
